TPU v7x, 512 devices: a whole 4x8x8 slice. The times are simulated.
512 devices in a mesh: expert: 8 (over z), dp: 16 (over y, core), section: 4 (over x).
Axes of the slice: x: 4, y: 8, z: 8, core: 2. Of those that a mesh axis runs over, the one named last changes fastest.
Arguments:
- active: bfloat16 [4, 4096, 2, 8192], P('section', ('expert', 'dp')), may hold values from -6 to 6
- out_grad: bfloat16 [4, 4096, 3072], P('section', ('expert', 'dp')), may hold values from -6 to 6
- proj_model: bfloat16 [64, 3072], P(None, 'dp'), may hold values from -0.109375 to 0.109375
- routes: int32 [4, 4096, 2], P('section', ('expert', 'dp')), may hold values from 0 to 7, all different within a row; in each aligned block of 32 rows (0 to 31, 32 to 63, ..., all dimensions but the last counted through in order) at most 16 rows name the same one
- route_weight: float32 [4, 4096, 2], P('section', ('expert', 'dp')), may hold values from 0.2 to 1
- seq_ids: int32 [4096], P(('expert', 'dp')), may hold values from 0 to 63, never falling along the last dimension, each value on 1 to 128 neighbouring positions
- proj_hidden: bfloat16 [8, 64, 8192], P('expert', None, 'dp'), may hold values from -0.0625 to 0.0625
- query_feat: bfloat16 [4, 8, 256, 4096], P('section', 'expert', 'dp'), may hold values from -0.00390625 to 0.00390625
Outputs:
- scores: float32 [64, 256], P(('expert', 'section'), 'dp')
Inputs may be any that keep to these rules, and one draw needn't show every extreme that they name: `routes`: each row names 2 different experts; among the 32 rows of one device at one checkpoint no expert is named by more than 16 rows, and in some device's rows one expert is named by exactly 16 rows. `seq_ids`: sequence numbers never fall along the tokens; each sequence has 1 to 128 tokens, one exactly 128.
All inputs are finite; a program needn't handle non-finite values.
Results may differ from a plain program's by a relative error of at most 0.0029.
Values may be sent and summed in bfloat16 or wider, within the bound.
No kernel may reach another device: no remote copies, remote signals or barrier semaphores. Data moves between devices by JAX's collectives and lax.ppermute only.
A program may use at most 64 MiB of HBM per device.

v0:
```python
import math
import jax
import jax.numpy as jnp
from jax import lax
from jax.sharding import PartitionSpec as P

SEQS = 64


def slot_table(route_block, experts, capacity):
    flat = route_block.reshape(-1)
    pairs = flat.shape[0]
    labels = jnp.arange(experts, dtype=jnp.int32)
    member = (flat[:, None] == labels[None, :]).astype(jnp.int32)
    before = jnp.cumsum(member, axis=0) - member
    position = jnp.sum(before * member, axis=1)
    slots = jnp.arange(capacity, dtype=jnp.int32)
    match = (flat[None, None, :] == labels[:, None, None]) & (
        position[None, None, :] == slots[None, :, None]
    )
    filled = jnp.any(match, axis=2)
    slot_index = jnp.sum(
        match.astype(jnp.int32) * jnp.arange(pairs, dtype=jnp.int32)[None, None, :], axis=2
    )
    return (slot_index, filled)


def seq_features(projected, vectors, sequence_rows, sequences):
    total_rows, rank = projected.shape
    block = math.gcd(total_rows, 256)
    labels = jnp.arange(sequences, dtype=jnp.int32)

    def step(running, begin):
        vector_part = vectors.astype(jnp.float32)
        member = (sequence_rows[:, None] == labels[None, :]).astype(jnp.float32)
        outer = (projected[:, :, None] * vector_part[:, None, :]).reshape(block, rank * rank)
        added = lax.dot_general(
            member, outer, (((0,), (0,)), ((), ())), precision=lax.Precision.HIGHEST
        )
        return (running + added, None)

    begins = jnp.arange(total_rows // block, dtype=jnp.int32) * block
    running, unused = lax.scan(step, jnp.zeros((sequences, rank * rank), jnp.float32), begins)
    return running


def on_device(active, out_grad, proj_model, routes, route_weight, seq_ids, proj_hidden, query_feat):
    experts = lax.axis_size("expert")
    holders = lax.axis_size("dp")
    tok_count = active.shape[1]
    top_count = active.shape[2]
    hidden_width = active.shape[3]
    rank = proj_model.shape[0]
    spread = experts * holders
    capacity = min(tok_count, holders * ((2 * top_count * tok_count + spread - 1) // spread))
    per_holder = capacity // holders
    model_full, hidden_full = (
        lax.all_gather(proj_model, "dp", axis=1, tiled=True),
        lax.all_gather(proj_hidden[0], "dp", axis=1, tiled=True),
    )
    dy_proj = lax.dot_general(
        out_grad[0], model_full, (((1,), (1,)), ((), ())), preferred_element_type=jnp.float32
    )
    scaled = (route_weight[0][:, :, None] * dy_proj[:, None, :]).astype(jnp.bfloat16)
    slot_index, filled = slot_table(routes[0], experts, capacity)
    pair_rows = active[0].reshape(-1, hidden_width)[slot_index]
    pair_vec = jnp.where(
        filled[:, :, None], scaled.reshape(-1, rank)[slot_index], jnp.zeros((), jnp.bfloat16)
    )
    pair_seq = seq_ids[slot_index // top_count]
    lead = (experts * holders, per_holder)
    moved_a, moved_v, moved_s = (
        lax.all_to_all(
            pair_rows.reshape(lead + (hidden_width,)),
            ("expert", "dp"),
            split_axis=0,
            concat_axis=0,
            tiled=True,
        ),
        lax.all_to_all(
            pair_vec.reshape(lead + (rank,)),
            ("expert", "dp"),
            split_axis=0,
            concat_axis=0,
            tiled=True,
        ),
        lax.all_to_all(
            pair_seq.reshape(lead), ("expert", "dp"), split_axis=0, concat_axis=0, tiled=True
        ),
    )
    act_rows = lax.dot_general(
        moved_a.reshape(-1, hidden_width),
        hidden_full,
        (((1,), (1,)), ((), ())),
        preferred_element_type=jnp.float32,
    )
    vector_rows = moved_v.reshape(-1, rank)
    sequence_rows = moved_s.reshape(-1)
    partial_feat = seq_features(act_rows, vector_rows, sequence_rows, SEQS)
    queries_here = query_feat[0, 0]
    partial_scores = lax.dot_general(
        partial_feat,
        lax.all_gather(queries_here, "dp", axis=0, tiled=True).astype(jnp.float32),
        (((1,), (1,)), ((), ())),
        precision=lax.Precision.HIGHEST,
    )
    shared = lax.psum_scatter(partial_scores, "dp", scatter_dimension=1, tiled=True)
    return lax.psum_scatter(shared, ("expert", "section"), scatter_dimension=0, tiled=True)


def solution(mesh):
    placed = (
        P("section", ("expert", "dp"), None, None),
        P("section", ("expert", "dp"), None),
        P(None, "dp"),
        P("section", ("expert", "dp"), None),
        P("section", ("expert", "dp"), None),
        P(("expert", "dp")),
        P("expert", None, "dp"),
        P("section", "expert", "dp", None),
    )
    return jax.shard_map(
        on_device,
        mesh=mesh,
        in_specs=placed,
        out_specs=P(("expert", "section"), "dp"),
        check_vma=False,
    )
```

profile of v0, /device:TPU:32, one launch (start us, length us, event | category | flops | bytes accessed | tf_op | source)
XLA Modules:
  0.0 300.5 jit_solution(10034062944627521986)
XLA Ops:
  6.5 0.7 all-gather.6.cloned.1.call-update
  7.3 0.8 copy.34
  8.9 1.2 gather_fusion
  10.1 0.7 copy.35
  10.8 17.0 %all-to-all-start = ((s32[128,1,1]{2,1,0:T(1,128)}), s32[128,1,1]{2,1,0:T(1,128)S(1)}, u32[]{:S(2)}, u32[]{:S(2)}) async-start(s32[128,1,1]{2,1,0:T(1,128)} %copy.35), calls=%async_computation | async-start | bytes 131072 | tf_op jit(solution)/shard_map/all_to_all | solution.py:87
  27.9 16.2 %all-gather.2 = bf16[16,192,64]{1,2,0:T(8,128)(2,1)S(1)} all-gather(bf16[1,192,64]{1,2,0:T(8,128)(2,1)S(1)} %bitcast.58), channel_id=1, replica_groups=mesh['expert'=8,'dp'=16,'section'=4] {'dp'}, dimensions={0}, use_global_device_ids=true | all-gather | bytes 417792 | tf_op jit(solution)/shard_map/all_gather | solution.py:58
  45.9 0.7 gather_fusion.2
  46.7 0.7 copy.39
  47.4 13.9 %all-to-all-start.2 = ((bf16[128,1,64]{2,1,0:T(2,128)(2,1)}), bf16[128,1,64]{2,1,0:T(2,128)(2,1)S(1)}, u32[]{:S(2)}, u32[]{:S(2)}) async-start(bf16[128,1,64]{2,1,0:T(2,128)(2,1)} %copy.39), calls=%async_computation.2 | async-start | bytes 131072 | tf_op jit(solution)/shard_map/all_to_all | solution.py:80
  61.8 1.9 gather_fusion.1
  64.1 2.9 reduce.1
  67.0 4.5 %reshape.218 = bf16[128,2,4096]{2,1,0:T(2,128)(2,1)} reshape(bf16[128,8192]{1,0:T(8,128)(2,1)} %reduce.1) | data formatting | bytes 4194304
  71.5 13.7 %all-to-all-start.1 = ((bf16[128,2,4096]{2,1,0:T(2,128)(2,1)}), bf16[128,2,4096]{2,1,0:T(2,128)(2,1)S(1)}, u32[]{:S(2)}, u32[]{:S(2)}) async-start(bf16[128,2,4096]{2,1,0:T(2,128)(2,1)} %reshape.218), calls=%async_computation.1 | async-start | bytes 4194304 | tf_op jit(solution)/shard_map/all_to_all | solution.py:73
  85.3 0.7 all-gather.8.cloned.1.call-update
  86.2 2.4 reduce
  88.7 56.5 %all-to-all-done.1 = bf16[128,2,4096]{2,1,0:T(2,128)(2,1)S(1)} async-done(((bf16[128,2,4096]{2,1,0:T(2,128)(2,1)}), bf16[128,2,4096]{2,1,0:T(2,128)(2,1)S(1)}, u32[]{:S(2)}, u32[]{:S(2)}) %all-to-all-start.1) | async-done | bytes 2097184 | tf_op jit(solution)/shard_map/all_to_all | solution.py:73
  145.2 6.8 %reshape.219 = bf16[128,1,8192]{2,1,0:T(2,128)(2,1)} reshape(bf16[128,2,4096]{2,1,0:T(2,128)(2,1)S(1)} %all-to-all-done.1) | data formatting | bytes 4194304
  152.0 4.9 %fusion = f32[128,64]{0,1:T(8,128)S(1)} fusion(bf16[128,1,8192]{2,1,0:T(2,128)(2,1)} %reshape.219, bf16[1,64,8192]{2,1,0:T(8,128)(2,1)} %all-gather.6.cloned.1.call-done), kind=kOutput, calls=%fused_computation.3 | convolution fusion | flops 134217728 | bytes 3178496 | tf_op jit(solution)/shard_map/dot_general | solution.py:91
  157.2 1.4 fusion.10
  158.6 4.0 %fusion.3 = f32[64,256]{0,1:T(8,128)} fusion(f32[64,4096]{1,0:T(8,128)S(1)} %fusion.10, bf16[1,1,256,4096]{3,2,1,0:T(8,128)(2,1)} %all-gather.8.cloned.1.call-done), kind=kOutput, calls=%fused_computation.6 | convolution fusion | flops 805306368 | bytes 3211264 | tf_op jit(solution)/shard_map/dot_general | solution.py:101
  162.6 1.3 dynamic-slice
  164.6 51.9 %reduce-scatter.3.cloned.1.call-done = f32[64,16]{0,1:T(8,128)} async-done(((f32[64,256]{0,1:T(8,128)}), f32[64,16]{0,1:T(8,128)}) %reduce-scatter.3.cloned.1.call-update) | async-done | bytes 4112 | tf_op jit(solution)/shard_map/reduce_scatter | solution.py:107
  216.4 76.8 %all-reduce = f32[64,16]{0,1:T(8,128)S(1)} all-reduce(f32[64,16]{0,1:T(8,128)} %reduce-scatter.3.cloned.1.call-done), channel_id=5, replica_groups=mesh['expert'=8,'dp'=16,'section'=4] {'expert','section'}, use_global_device_ids=true, to_apply=%region_5.6.clone | all-reduce | flops 1024 | bytes 8192
  293.3 0.6 copy.41
  (46 shorter events, 4.4 us)
Async XLA Ops:
  6.5 39.0 %copy-start = (bf16[1,32,3072]{2,1,0:T(8,128)(2,1)S(1)}, bf16[1,32,3072]{2,1,0:T(8,128)(2,1)}, u32[]{:S(2)}) copy-start(bf16[1,32,3072]{2,1,0:T(8,128)(2,1)} %param.9) | copy-start | bytes 589828
  6.5 2.3 copy-start.1
  6.5 145.5 %all-gather.6.cloned.1.call-start = ((), (), s32[]{:S(2)}) async-start(), calls=%async_computation.5 | async-start | bytes 1114112 | tf_op jit(solution)/shard_map/all_gather | solution.py:59
  8.9 19.0 %copy-start.3 = (bf16[64,192]{1,0:T(8,128)(2,1)S(1)}, bf16[64,192]{1,0:T(8,128)(2,1)}, u32[]{:S(2)}) copy-start(bf16[64,192]{1,0:T(8,128)(2,1)} %param.10) | copy-start | bytes 73732
  10.1 35.2 %copy-start.4 = (f32[1,32,2]{1,2,0:T(2,128)S(1)}, f32[1,32,2]{1,2,0:T(2,128)}, u32[]{:S(2)}) copy-start(f32[1,32,2]{1,2,0:T(2,128)} %param.12) | copy-start | bytes 772
  10.1 51.2 %copy-start.2 = (bf16[1,32,2,8192]{3,2,1,0:T(2,128)(2,1)S(1)}, bf16[1,32,2,8192]{3,2,1,0:T(2,128)(2,1)}, u32[]{:S(2)}) copy-start(bf16[1,32,2,8192]{3,2,1,0:T(2,128)(2,1)} %param.8) | copy-start | bytes 3145732
  10.8 36.6 %all-to-all-start = ((s32[128,1,1]{2,1,0:T(1,128)}), s32[128,1,1]{2,1,0:T(1,128)S(1)}, u32[]{:S(2)}, u32[]{:S(2)}) async-start(s32[128,1,1]{2,1,0:T(1,128)} %copy.35), calls=%async_computation | async-start | bytes 131072 | tf_op jit(solution)/shard_map/all_to_all | solution.py:87
  47.4 24.1 %all-to-all-start.2 = ((bf16[128,1,64]{2,1,0:T(2,128)(2,1)}), bf16[128,1,64]{2,1,0:T(2,128)(2,1)S(1)}, u32[]{:S(2)}, u32[]{:S(2)}) async-start(bf16[128,1,64]{2,1,0:T(2,128)(2,1)} %copy.39), calls=%async_computation.2 | async-start | bytes 131072 | tf_op jit(solution)/shard_map/all_to_all | solution.py:80
  71.5 73.7 %all-to-all-start.1 = ((bf16[128,2,4096]{2,1,0:T(2,128)(2,1)}), bf16[128,2,4096]{2,1,0:T(2,128)(2,1)S(1)}, u32[]{:S(2)}, u32[]{:S(2)}) async-start(bf16[128,2,4096]{2,1,0:T(2,128)(2,1)} %reshape.218), calls=%async_computation.1 | async-start | bytes 4194304 | tf_op jit(solution)/shard_map/all_to_all | solution.py:73
  85.2 73.3 %all-gather.8.cloned.1.call-start = ((), (), s32[]{:S(2)}) async-start(), calls=%async_computation.6 | async-start | bytes 2228224 | tf_op jit(solution)/shard_map/all_gather | solution.py:103
  86.0 130.4 %reduce-scatter.3.cloned.1.call-start = ((), (), s32[]{:S(2)}) async-start(), calls=%async_computation.4 | async-start | bytes 139264 | tf_op jit(solution)/shard_map/reduce_scatter | solution.py:107
Sparse Core Ops, SparseCore 0:
  9.5 43.3 all-gather.5
  88.2 52.9 all-gather.7
  162.8 53.6 reduce-scatter.2
where the time goes:
time: 301 us
  waiting for transfers between devices  110 us (37%)
  blocking collectives  93.1 us (31%)
  starting transfers between devices  44.9 us (15%)
  local copies, waits for them, and re-layouts  21.7 us (7%)
  between operations  14 us (5%)
  matrix products  10.5 us (3%)
  other arithmetic  6.55 us (2%)
    unnamed x1, blocking collectives  76.8 us
    all_to_all x1, waiting for transfers between devices, on_device(): lax.all_to_all(pair_rows.reshape(lead + (hidden_width,)), ('expert', 'dp'...  56.5 us
    reduce_scatter x1, waiting for transfers between devices, on_device(): lax.psum_scatter(partial_scores, 'dp', scatter_dimension=1, tiled=True)  51.9 us
    all_to_all x1, starting transfers between devices, on_device(): lax.all_to_all(pair_seq.reshape(lead), ('expert', 'dp'), split_axis=0, co...  17 us
    all_gather x1, blocking collectives, on_device(): lax.all_gather(proj_model, 'dp', axis=1, tiled=True)  16.2 us
    unnamed x17, local copies, waits for them, and re-layouts  14 us
    all_to_all x1, starting transfers between devices, on_device(): lax.all_to_all(pair_vec.reshape(lead + (rank,)), ('expert', 'dp'), split_...  13.9 us
    all_to_all x1, starting transfers between devices, on_device(): lax.all_to_all(pair_rows.reshape(lead + (hidden_width,)), ('expert', 'dp'...  13.7 us
  transfers between devices with their start and end apart: 6, of which 2 were waited for; matrix products, arithmetic and copies ran while one was open for 11% of the time, Pallas kernels for 0%

commit v1 on v0

--- a/solution.py
+++ b/solution.py
@@ -55,7 +55,7 @@
     capacity = min(tok_count, holders * ((2 * top_count * tok_count + spread - 1) // spread))
     per_holder = capacity // holders
     model_full, hidden_full = (
-        lax.all_gather(proj_model, "dp", axis=1, tiled=True),
+        jnp.concatenate(lax.all_gather(proj_model, "dp"), axis=1),
         lax.all_gather(proj_hidden[0], "dp", axis=1, tiled=True),
     )
     dy_proj = lax.dot_general(

time: 301 us -> 301 us (level)
    unnamed x17 -> x16, local copies, waits for them, and re-layouts: 14 us -> 13.5 us
where the time goes in v1:
time: 301 us
  waiting for transfers between devices  110 us (37%)
  blocking collectives  93.1 us (31%)
  starting transfers between devices  44.9 us (15%)
  local copies, waits for them, and re-layouts  21.7 us (7%)
  between operations  14 us (5%)
  matrix products  10.5 us (3%)
  other arithmetic  6.55 us (2%)
    unnamed x1, blocking collectives  76.8 us
    all_to_all x1, waiting for transfers between devices, on_device(): lax.all_to_all(pair_rows.reshape(lead + (hidden_width,)), ('expert', 'dp'...  56.5 us
    reduce_scatter x1, waiting for transfers between devices, on_device(): lax.psum_scatter(partial_scores, 'dp', scatter_dimension=1, tiled=True)  51.9 us
    all_to_all x1, starting transfers between devices, on_device(): lax.all_to_all(pair_seq.reshape(lead), ('expert', 'dp'), split_axis=0, co...  17 us
    all_gather x1, blocking collectives, on_device(): lax.all_gather(proj_model, 'dp')  16.2 us
    all_to_all x1, starting transfers between devices, on_device(): lax.all_to_all(pair_vec.reshape(lead + (rank,)), ('expert', 'dp'), split_...  13.9 us
    all_to_all x1, starting transfers between devices, on_device(): lax.all_to_all(pair_rows.reshape(lead + (hidden_width,)), ('expert', 'dp'...  13.7 us
    unnamed x16, local copies, waits for them, and re-layouts  13.5 us
  transfers between devices with their start and end apart: 6, of which 2 were waited for; matrix products, arithmetic and copies ran while one was open for 11% of the time, Pallas kernels for 0%

profile of v1, /device:TPU:32, one launch (start us, length us, event | category | flops | bytes accessed | tf_op | source)
XLA Modules:
  0.0 300.5 jit_solution(14644986373049556219)
XLA Ops:
  6.5 0.7 all-gather.6.cloned.1.call-update
  7.3 0.8 copy.34
  8.9 1.2 gather_fusion
  10.1 0.7 copy.35
  10.8 17.0 %all-to-all-start = ((s32[128,1,1]{2,1,0:T(1,128)}), s32[128,1,1]{2,1,0:T(1,128)S(1)}, u32[]{:S(2)}, u32[]{:S(2)}) async-start(s32[128,1,1]{2,1,0:T(1,128)} %copy.35), calls=%async_computation | async-start | bytes 131072 | tf_op jit(solution)/shard_map/all_to_all | solution.py:87
  27.9 16.2 %all-gather.1 = bf16[1024,192]{1,0:T(8,128)(2,1)S(1)} all-gather(bf16[64,192]{1,0:T(8,128)(2,1)S(1)} %copy-done.3), channel_id=3, replica_groups=mesh['expert'=8,'dp'=16,'section'=4] {'dp'}, dimensions={0}, use_global_device_ids=true | all-gather | bytes 417792 | tf_op jit(solution)/shard_map/all_gather | solution.py:58
  45.9 0.7 gather_fusion.2
  46.7 0.7 copy.39
  47.4 13.9 %all-to-all-start.2 = ((bf16[128,1,64]{2,1,0:T(2,128)(2,1)}), bf16[128,1,64]{2,1,0:T(2,128)(2,1)S(1)}, u32[]{:S(2)}, u32[]{:S(2)}) async-start(bf16[128,1,64]{2,1,0:T(2,128)(2,1)} %copy.39), calls=%async_computation.2 | async-start | bytes 131072 | tf_op jit(solution)/shard_map/all_to_all | solution.py:80
  61.8 1.9 gather_fusion.1
  64.1 2.9 reduce.1
  67.0 4.5 %reshape.225 = bf16[128,2,4096]{2,1,0:T(2,128)(2,1)} reshape(bf16[128,8192]{1,0:T(8,128)(2,1)} %reduce.1) | data formatting | bytes 4194304
  71.5 13.7 %all-to-all-start.1 = ((bf16[128,2,4096]{2,1,0:T(2,128)(2,1)}), bf16[128,2,4096]{2,1,0:T(2,128)(2,1)S(1)}, u32[]{:S(2)}, u32[]{:S(2)}) async-start(bf16[128,2,4096]{2,1,0:T(2,128)(2,1)} %reshape.225), calls=%async_computation.1 | async-start | bytes 4194304 | tf_op jit(solution)/shard_map/all_to_all | solution.py:73
  85.3 0.7 all-gather.8.cloned.1.call-update
  86.2 2.4 reduce
  88.7 56.5 %all-to-all-done.1 = bf16[128,2,4096]{2,1,0:T(2,128)(2,1)S(1)} async-done(((bf16[128,2,4096]{2,1,0:T(2,128)(2,1)}), bf16[128,2,4096]{2,1,0:T(2,128)(2,1)S(1)}, u32[]{:S(2)}, u32[]{:S(2)}) %all-to-all-start.1) | async-done | bytes 2097184 | tf_op jit(solution)/shard_map/all_to_all | solution.py:73
  145.2 6.8 %reshape.226 = bf16[128,1,8192]{2,1,0:T(2,128)(2,1)} reshape(bf16[128,2,4096]{2,1,0:T(2,128)(2,1)S(1)} %all-to-all-done.1) | data formatting | bytes 4194304
  152.0 4.9 %fusion = f32[128,64]{0,1:T(8,128)S(1)} fusion(bf16[128,1,8192]{2,1,0:T(2,128)(2,1)} %reshape.226, bf16[1,64,8192]{2,1,0:T(8,128)(2,1)} %all-gather.6.cloned.1.call-done), kind=kOutput, calls=%fused_computation.3 | convolution fusion | flops 134217728 | bytes 3178496 | tf_op jit(solution)/shard_map/dot_general | solution.py:91
  157.2 1.4 fusion.10
  158.6 4.0 %fusion.3 = f32[64,256]{0,1:T(8,128)} fusion(f32[64,4096]{1,0:T(8,128)S(1)} %fusion.10, bf16[1,1,256,4096]{3,2,1,0:T(8,128)(2,1)} %all-gather.8.cloned.1.call-done), kind=kOutput, calls=%fused_computation.6 | convolution fusion | flops 805306368 | bytes 3211264 | tf_op jit(solution)/shard_map/dot_general | solution.py:101
  162.6 1.3 dynamic-slice
  164.6 51.9 %reduce-scatter.3.cloned.1.call-done = f32[64,16]{0,1:T(8,128)} async-done(((f32[64,256]{0,1:T(8,128)}), f32[64,16]{0,1:T(8,128)}) %reduce-scatter.3.cloned.1.call-update) | async-done | bytes 4112 | tf_op jit(solution)/shard_map/reduce_scatter | solution.py:107
  216.4 76.8 %all-reduce = f32[64,16]{0,1:T(8,128)S(1)} all-reduce(f32[64,16]{0,1:T(8,128)} %reduce-scatter.3.cloned.1.call-done), channel_id=6, replica_groups=mesh['expert'=8,'dp'=16,'section'=4] {'expert','section'}, use_global_device_ids=true, to_apply=%region_5.6.clone | all-reduce | flops 1024 | bytes 8192
  293.3 0.6 copy.41
  (46 shorter events, 4.4 us)
Async XLA Ops:
  6.5 39.0 %copy-start = (bf16[1,32,3072]{2,1,0:T(8,128)(2,1)S(1)}, bf16[1,32,3072]{2,1,0:T(8,128)(2,1)}, u32[]{:S(2)}) copy-start(bf16[1,32,3072]{2,1,0:T(8,128)(2,1)} %param.9) | copy-start | bytes 589828
  6.5 2.3 copy-start.1
  6.5 145.5 %all-gather.6.cloned.1.call-start = ((), (), s32[]{:S(2)}) async-start(), calls=%async_computation.5 | async-start | bytes 1114112 | tf_op jit(solution)/shard_map/all_gather | solution.py:59
  8.9 19.0 %copy-start.3 = (bf16[64,192]{1,0:T(8,128)(2,1)S(1)}, bf16[64,192]{1,0:T(8,128)(2,1)}, u32[]{:S(2)}) copy-start(bf16[64,192]{1,0:T(8,128)(2,1)} %param.10) | copy-start | bytes 73732
  10.1 35.2 %copy-start.4 = (f32[1,32,2]{1,2,0:T(2,128)S(1)}, f32[1,32,2]{1,2,0:T(2,128)}, u32[]{:S(2)}) copy-start(f32[1,32,2]{1,2,0:T(2,128)} %param.12) | copy-start | bytes 772
  10.1 51.2 %copy-start.2 = (bf16[1,32,2,8192]{3,2,1,0:T(2,128)(2,1)S(1)}, bf16[1,32,2,8192]{3,2,1,0:T(2,128)(2,1)}, u32[]{:S(2)}) copy-start(bf16[1,32,2,8192]{3,2,1,0:T(2,128)(2,1)} %param.8) | copy-start | bytes 3145732
  10.8 36.6 %all-to-all-start = ((s32[128,1,1]{2,1,0:T(1,128)}), s32[128,1,1]{2,1,0:T(1,128)S(1)}, u32[]{:S(2)}, u32[]{:S(2)}) async-start(s32[128,1,1]{2,1,0:T(1,128)} %copy.35), calls=%async_computation | async-start | bytes 131072 | tf_op jit(solution)/shard_map/all_to_all | solution.py:87
  47.4 24.1 %all-to-all-start.2 = ((bf16[128,1,64]{2,1,0:T(2,128)(2,1)}), bf16[128,1,64]{2,1,0:T(2,128)(2,1)S(1)}, u32[]{:S(2)}, u32[]{:S(2)}) async-start(bf16[128,1,64]{2,1,0:T(2,128)(2,1)} %copy.39), calls=%async_computation.2 | async-start | bytes 131072 | tf_op jit(solution)/shard_map/all_to_all | solution.py:80
  71.5 73.7 %all-to-all-start.1 = ((bf16[128,2,4096]{2,1,0:T(2,128)(2,1)}), bf16[128,2,4096]{2,1,0:T(2,128)(2,1)S(1)}, u32[]{:S(2)}, u32[]{:S(2)}) async-start(bf16[128,2,4096]{2,1,0:T(2,128)(2,1)} %reshape.225), calls=%async_computation.1 | async-start | bytes 4194304 | tf_op jit(solution)/shard_map/all_to_all | solution.py:73
  85.2 73.3 %all-gather.8.cloned.1.call-start = ((), (), s32[]{:S(2)}) async-start(), calls=%async_computation.6 | async-start | bytes 2228224 | tf_op jit(solution)/shard_map/all_gather | solution.py:103
  86.0 130.4 %reduce-scatter.3.cloned.1.call-start = ((), (), s32[]{:S(2)}) async-start(), calls=%async_computation.4 | async-start | bytes 139264 | tf_op jit(solution)/shard_map/reduce_scatter | solution.py:107
Sparse Core Ops, SparseCore 0:
  9.5 43.3 all-gather.5
  88.2 52.9 all-gather.7
  162.8 53.6 reduce-scatter.2
